TPU v7x, 32 devices: a whole 2x2x4 slice. The times are simulated.
32 devices in a mesh: lon: 8 (over z, x), lat: 4 (over y, core).
Axes of the slice: x: 2, y: 2, z: 4, core: 2. Of those that a mesh axis runs over, the one named last changes fastest.
Arguments:
- inputs: bfloat16 [256, 32, 2048], P(None, 'lat', 'lon'), may hold values from -6 to 6
- cotangent: bfloat16 [256, 32, 2048], P(None, 'lat', 'lon'), may hold values from -6 to 6
- mixing: bfloat16 [9, 256, 256], replicated, may hold values from -0.125 to 0.125
- filters: bfloat16 [9, 32, 3, 33], P(None, 'lat'), may hold values from -0.8984375 to 0.8984375
- support: int32 [32], P('lat'), may hold values from 1 to 16, as said below
Outputs:
- input_grad: bfloat16 [256, 32, 2048], P(None, 'lat', 'lon')
- weight_grad: float32 [9, 256, 256], replicated
Inputs may be any that keep to these rules, and one draw needn't show every extreme that they name: support[i] is the widest longitude offset, in cells, reached by the filter of latitude row i.
All inputs are finite; a program needn't handle non-finite values.
Results may differ from a plain program's by a relative error of at most 0.0051.
Values may be sent and summed in bfloat16 or wider, within the bound.
A program may use at most 192 MiB of HBM per device.

v0:
```python
import math
import jax
import jax.numpy as jnp
from jax import lax
from jax.sharding import PartitionSpec as P

LAT_REACH = 1
LON_REACH = 16


def with_halo(cells, sides, width, closed):
    for axis, dim in sides:
        count = lax.axis_size(axis)
        ends = count if closed else count - 1
        head = lax.slice_in_dim(cells, 0, width, axis=dim)
        tail = lax.slice_in_dim(cells, cells.shape[dim] - width, cells.shape[dim], axis=dim)
        cells = jnp.concatenate(
            [
                lax.ppermute(tail, axis, [(i, (i + 1) % count) for i in range(ends)]),
                cells,
                lax.ppermute(head, axis, [((i + 1) % count, i) for i in range(ends)]),
            ],
            axis=dim,
        )
    return cells


def spread_block(source, coef_source, row_first, rows, col_first, cols):
    kernels = coef_source.shape[0]
    chans = source.shape[0]
    span = LON_REACH
    reach = LAT_REACH
    tap_count = 2 * span + 1
    window = cols + 2 * span
    tap_axis = jnp.arange(tap_count, dtype=jnp.int32)[:, None, None]
    wide_axis = jnp.arange(window, dtype=jnp.int32)[None, :, None]
    cell_axis = jnp.arange(cols, dtype=jnp.int32)[None, None, :]
    selector = (cell_axis + 2 * span - wide_axis == tap_axis).astype(jnp.bfloat16)
    total = jnp.zeros((kernels, chans, rows, cols), jnp.float32)
    for offset in range(2 * reach + 1):
        start = row_first + 2 * reach - offset
        rows_in = source[:, start : start + rows, col_first : col_first + window]
        part_coefs = coef_source[:, start : start + rows, offset, :]
        tiles = jnp.einsum(
            "bpq,kib->kipq", selector, part_coefs, preferred_element_type=jnp.float32
        ).astype(jnp.bfloat16)
        total = total + jnp.einsum(
            "oip,kipq->koiq", rows_in, tiles, preferred_element_type=jnp.float32
        )
    return total.astype(jnp.bfloat16)


def local(inputs, cotangent, mixing, filters, support):
    chans, lat_rows, lon_cols = inputs.shape
    span = LON_REACH
    reach = LAT_REACH
    tap_count = 2 * span + 1
    offsets = jnp.arange(tap_count, dtype=jnp.int32) - span
    keep = (jnp.abs(offsets)[None, :] <= support[:, None]).astype(jnp.bfloat16)
    coefs = filters * keep[None, :, None, :]
    widened = with_halo(cotangent, (("lon", 2),), span, True)
    padded = with_halo(widened, (("lat", 1),), reach, False)
    coef_pad = with_halo(coefs, (("lat", 1),), reach, False)
    spread = spread_block(padded, coef_pad, 0, lat_rows, 0, lon_cols)
    local_grad = jnp.einsum("koiq,ciq->koc", spread, inputs, preferred_element_type=jnp.float32)
    total_cells = lat_rows * lax.axis_size("lat") * lon_cols * lax.axis_size("lon")
    weight_grad = lax.psum(local_grad, ("lon", "lat")) * (1.0 / math.sqrt(total_cells))
    input_grad = jnp.einsum(
        "koc,koiq->ciq", mixing, spread, preferred_element_type=jnp.float32
    ).astype(jnp.bfloat16)
    return (input_grad, weight_grad)


def solution(mesh):
    return jax.shard_map(
        local,
        mesh=mesh,
        in_specs=(
            P(None, "lat", "lon"),
            P(None, "lat", "lon"),
            P(),
            P(None, "lat", None, None),
            P("lat"),
        ),
        out_specs=(P(None, "lat", "lon"), P()),
        check_vma=False,
    )
```

profile of v0, /device:TPU:0, one launch (start us, length us, event | category | flops | bytes accessed | tf_op | source)
XLA Modules:
  0.0 247.0 jit_solution(17493707170582099157)
XLA Ops:
  7.2 0.0 copy-start
  7.2 0.0 copy-start.2
  7.2 0.0 copy-start.1
  7.2 0.0 all-reduce.2.cloned.1.call-start
  7.2 1.7 copy.7
  9.0 3.0 %collective-permute-start.1 = (bf16[256,8,16]{0,2,1:T(8,128)(2,1)S(1)}, bf16[256,8,16]{0,2,1:T(8,128)(2,1)S(1)}, u32[]{:S(2)}, u32[]{:S(2)}) collective-permute-start(bf16[256,8,16]{0,2,1:T(8,128)(2,1)S(1)} %get-tuple-element.6), channel_id=1, source_target_pairs={{0,4},{4,8},{8,12},{12,16},{16,20},{20,24},{24,28},{28,0},{1,5},{5... | collective-permute-start | bytes 196616 | tf_op jit(solution)/shard_map/ppermute | solution.py:19
  12.0 3.1 %collective-permute-start.2 = (bf16[256,8,16]{0,2,1:T(8,128)(2,1)S(1)}, bf16[256,8,16]{0,2,1:T(8,128)(2,1)S(1)}, u32[]{:S(2)}, u32[]{:S(2)}) collective-permute-start(bf16[256,8,16]{0,2,1:T(8,128)(2,1)S(1)} %get-tuple-element.7), channel_id=1, source_target_pairs={{4,0},{8,4},{12,8},{16,12},{20,16},{24,20},{28,24},{0,28},{5,1},{9... | collective-permute-start | bytes 196616 | tf_op jit(solution)/shard_map/ppermute | solution.py:21
  15.1 0.0 copy-done.2
  15.1 0.1 compare_convert_fusion
  15.2 0.0 copy-done.1
  15.2 1.3 collective-permute-start
  16.5 3.0 %collective-permute-start.4 = (bf16[9,1,3,33]{3,1,2,0:T(2,128)(2,1)S(1)}, bf16[9,1,3,33]{3,1,2,0:T(2,128)(2,1)S(1)}, u32[]{:S(2)}, u32[]{:S(2)}) collective-permute-start(bf16[9,1,3,33]{3,1,2,0:T(2,128)(2,1)S(1)} %get-tuple-element.8), channel_id=1, source_target_pairs={{0,1},{1,2},{2,3},{4,5},{5,6},{6,7},{8,9},{9,10},{10,11},{12,13},{... | collective-permute-start | bytes 5354 | tf_op jit(solution)/shard_map/ppermute | solution.py:19
  19.6 1.3 fusion.3
  20.9 6.6 %fusion.7 = bf16[9,8,288,256]{3,1,2,0:T(8,128)(2,1)} fusion(pred[33,288,256,1]{2,1,0,3:T(32,128)(4,1)S(1)} %fusion.3, bf16[9,8,3,33]{3,1,2,0:T(8,128)(2,1)S(1)} %broadcast_multiply_fusion.1), kind=kOutput, calls=%fused_computation.12 | convolution fusion | flops 350355456 | bytes 13068288 | tf_op jit(solution)/shard_map/bpq,kib->kipq/dot_general | solution.py:44
  27.5 0.0 collective-permute-done
  27.5 6.6 %fusion.9 = bf16[9,8,288,256]{3,1,2,0:T(8,128)(2,1)} fusion(pred[33,288,256,1]{2,1,0,3:T(32,128)(4,1)S(1)} %fusion.3, bf16[9,1,3,33]{3,1,2,0:T(2,128)(2,1)S(1)} %collective-permute-done, bf16[9,8,3,33]{3,1,2,0:T(8,128)(2,1)S(1)} %broadcast_multiply_fusion.1), kind=kOutput, calls=%fused_computation.14 | convolution fusion | flops 350364960 | bytes 13065894 | tf_op jit(solution)/shard_map/bpq,kib->kipq/dot_general | solution.py:44
  34.1 0.0 collective-permute-done.4
  34.1 6.6 %fusion.5 = bf16[9,8,288,256]{3,1,2,0:T(8,128)(2,1)} fusion(pred[33,288,256,1]{2,1,0,3:T(32,128)(4,1)S(1)} %fusion.3, bf16[9,8,3,33]{3,1,2,0:T(8,128)(2,1)S(1)} %broadcast_multiply_fusion.1, bf16[9,1,3,33]{3,1,2,0:T(2,128)(2,1)S(1)} %collective-permute-done.4), kind=kOutput, calls=%fused_computation.10 | convolution fusion | flops 350364960 | bytes 13065894 | tf_op jit(solution)/shard_map/bpq,kib->kipq/dot_general | solution.py:44
  40.7 0.0 collective-permute-done.1
  40.7 0.0 collective-permute-done.2
  40.7 0.1 pad_maximum_fusion.10
  40.8 0.0 slice-start
  40.8 0.7 fusion.31
  41.5 1.4 collective-permute-start.3
  42.9 0.0 slice-start.1
  43.0 0.0 slice-start.2
  43.0 4.7 %collective-permute-start.5 = (bf16[256,1,288]{0,2,1:T(8,128)(2,1)}, bf16[256,1,288]{0,2,1:T(8,128)(2,1)}, u32[]{:S(2)}, u32[]{:S(2)}) collective-permute-start(bf16[256,1,288]{0,2,1:T(8,128)(2,1)} %get-tuple-element.4), channel_id=1, source_target_pairs={{0,1},{1,2},{2,3},{4,5},{5,6},{6,7},{8,9},{9,10},{10,11},{12,13},{... | collective-permute-start | bytes 442376 | tf_op jit(solution)/shard_map/ppermute | solution.py:19
  47.7 12.9 %fusion.1 = f32[8,9,256,256]{3,2,1,0:T(8,128)} fusion(bf16[9,8,288,256]{3,1,2,0:T(8,128)(2,1)} %fusion.7, bf16[256,8,16]{0,2,1:T(8,128)(2,1)S(1)} %collective-permute-done.2, bf16[256,8,256]{0,2,1:T(8,128)(2,1)S(1)} %copy.7, bf16[256,8,16]{0,2,1:T(8,128)(2,1)S(1)} %collective-permute-done.1), kind=kOutput, calls=%fused_computation.5 | convolution fusion | flops 2721447936 | bytes 30670848 | tf_op jit(solution)/shard_map/oip,kipq->koiq/dot_general | solution.py:47
  60.6 0.0 collective-permute-done.3
  60.6 0.0 slice-done
  60.6 0.0 slice-done.1
  60.6 0.0 slice-done.2
  60.6 12.4 %fusion = f32[8,9,256,256]{3,2,1,0:T(8,128)} fusion(bf16[9,8,288,256]{3,1,2,0:T(8,128)(2,1)S(1)} %bitcast.53, bf16[256,1,288]{0,2,1:T(8,128)(2,1)} %collective-permute-done.3, bf16[256,8,16]{0,2,1:T(8,128)(2,1)S(1)} %collective-permute-done.2, bf16[256,8,256]{0,2,1:T(8,128)(2,1)S(1)} %copy.7, bf16[256,8,16]{0,2,1:T(8,128)(2,1)S(1)} %collective-permute-done.1), kind=kOutput, calls=%fused_computation.4 | convolution fusion | flops 2722627584 | bytes 30818304 | tf_op jit(solution)/shard_map/oip,kipq->koiq/dot_general | solution.py:47
  73.0 0.0 copy-start.3
  73.0 0.0 collective-permute-done.5
  73.0 21.8 %fusion.4 = bf16[9,256,8,256]{1,3,0,2:T(8,128)(2,1)} fusion(f32[8,9,256,256]{3,2,1,0:T(8,128)} %fusion, f32[8,9,256,256]{3,2,1,0:T(8,128)} %fusion.1, bf16[9,8,288,256]{3,1,2,0:T(8,128)(2,1)} %fusion.5, bf16[256,1,288]{0,2,1:T(8,128)(2,1)} %collective-permute-done.5, bf16[256,8,16]{0,2,1:T(8,128)(2,1)S(1)} %collective-permute-done.2, ...), kind=kOutput, calls=%fused_computation.9 | convolution fusion | flops 2736783360 | bytes 59129856 | tf_op jit(solution)/shard_map/oip,kipq->koiq/dot_general | solution.py:47
  94.8 0.0 copy-done.3
  94.8 7.8 %convolution_bitcast_fusion = f32[9,256,256]{2,1,0:T(8,128)} fusion(bf16[9,256,8,256]{1,3,0,2:T(8,128)(2,1)} %fusion.4, bf16[256,8,256,1]{2,1,0,3:T(8,128)(2,1)S(1)} %bitcast.54), kind=kOutput, calls=%fused_computation.17 | convolution fusion | flops 2415919104 | bytes 12845056 | tf_op jit(solution)/shard_map/koiq,ciq->koc/dot_general | solution.py:65
  102.6 0.0 all-reduce.2.cloned.1.call-update
  102.6 0.0 copy-done
  102.6 6.3 %fusion.11 = bf16[256,8,256]{0,2,1:T(8,128)(2,1)S(1)} fusion(bf16[9,256,8,256]{1,3,0,2:T(8,128)(2,1)} %fusion.4, bf16[9,256,256]{2,1,0:T(8,128)(2,1)S(1)} %copy-done), kind=kOutput, calls=%fused_computation.18 | convolution fusion | flops 2416443392 | bytes 11665408 | tf_op jit(solution)/shard_map/koc,koiq->ciq/dot_general | solution.py:68
  109.0 1.8 copy.12
  110.8 126.1 %all-reduce.2.cloned.1.call-done = f32[9,256,256]{2,1,0:T(8,128)} async-done(((f32[9,256,256]{2,1,0:T(8,128)}), f32[9,256,256]{2,1,0:T(8,128)}) %all-reduce.2.cloned.1.call-update) | async-done | bytes 2359312 | tf_op jit(solution)/shard_map/psum | solution.py:67
  236.8 3.3 %broadcast_multiply_fusion = f32[9,256,256]{2,1,0:T(8,128)} fusion(f32[9,256,256]{2,1,0:T(8,128)} %all-reduce.2.cloned.1.call-done), kind=kLoop, calls=%fused_computation.32 | loop fusion | flops 589824 | bytes 4718592 | tf_op jit(solution)/shard_map/mul | solution.py:67
  (7 shorter events, 0.1 us)
Async XLA Ops:
  7.2 95.5 %copy-start = (bf16[9,256,256]{2,1,0:T(8,128)(2,1)S(1)}, bf16[9,256,256]{2,1,0:T(8,128)(2,1)}, u32[]{:S(2)}) copy-start(bf16[9,256,256]{2,1,0:T(8,128)(2,1)} %param.7) | copy-start | bytes 3538948
  7.2 7.9 %copy-start.2 = (s32[8]{0:T(128)S(1)}, s32[8]{0:T(128)}, u32[]{:S(2)}) copy-start(s32[8]{0:T(128)} %param.9) | copy-start | bytes 100
  7.2 8.0 %copy-start.1 = (bf16[9,8,3,33]{3,1,2,0:T(8,128)(2,1)S(1)}, bf16[9,8,3,33]{3,1,2,0:T(8,128)(2,1)}, u32[]{:S(2)}) copy-start(bf16[9,8,3,33]{3,1,2,0:T(8,128)(2,1)} %param.8) | copy-start | bytes 42772
  7.2 229.6 %all-reduce.2.cloned.1.call-start = ((), (), s32[]{:S(2)}) async-start(), calls=%async_computation | async-start | bytes 4718592 | tf_op jit(solution)/shard_map/psum | solution.py:67
  9.0 31.7 %collective-permute-start.1 = (bf16[256,8,16]{0,2,1:T(8,128)(2,1)S(1)}, bf16[256,8,16]{0,2,1:T(8,128)(2,1)S(1)}, u32[]{:S(2)}, u32[]{:S(2)}) collective-permute-start(bf16[256,8,16]{0,2,1:T(8,128)(2,1)S(1)} %get-tuple-element.6), channel_id=1, source_target_pairs={{0,4},{4,8},{8,12},{12,16},{16,20},{20,24},{24,28},{28,0},{1,5},{5... | collective-permute-start | bytes 196616 | tf_op jit(solution)/shard_map/ppermute | solution.py:19
  12.0 28.7 %collective-permute-start.2 = (bf16[256,8,16]{0,2,1:T(8,128)(2,1)S(1)}, bf16[256,8,16]{0,2,1:T(8,128)(2,1)S(1)}, u32[]{:S(2)}, u32[]{:S(2)}) collective-permute-start(bf16[256,8,16]{0,2,1:T(8,128)(2,1)S(1)} %get-tuple-element.7), channel_id=1, source_target_pairs={{4,0},{8,4},{12,8},{16,12},{20,16},{24,20},{28,24},{0,28},{5,1},{9... | collective-permute-start | bytes 196616 | tf_op jit(solution)/shard_map/ppermute | solution.py:21
  15.2 12.3 %collective-permute-start = (bf16[9,1,3,33]{3,1,2,0:T(2,128)(2,1)S(1)}, bf16[9,1,3,33]{3,1,2,0:T(2,128)(2,1)S(1)}, u32[]{:S(2)}, u32[]{:S(2)}) collective-permute-start(bf16[9,1,3,33]{3,1,2,0:T(2,128)(2,1)S(1)} %get-tuple-element.9), channel_id=1, source_target_pairs={{1,0},{2,1},{3,2},{5,4},{6,5},{7,6},{9,8},{10,9},{11,10},{13,12},{... | collective-permute-start | bytes 5354 | tf_op jit(solution)/shard_map/ppermute | solution.py:21
  16.5 17.5 %collective-permute-start.4 = (bf16[9,1,3,33]{3,1,2,0:T(2,128)(2,1)S(1)}, bf16[9,1,3,33]{3,1,2,0:T(2,128)(2,1)S(1)}, u32[]{:S(2)}, u32[]{:S(2)}) collective-permute-start(bf16[9,1,3,33]{3,1,2,0:T(2,128)(2,1)S(1)} %get-tuple-element.8), channel_id=1, source_target_pairs={{0,1},{1,2},{2,3},{4,5},{5,6},{6,7},{8,9},{9,10},{10,11},{12,13},{... | collective-permute-start | bytes 5354 | tf_op jit(solution)/shard_map/ppermute | solution.py:19
  40.8 19.8 %slice-start = ((s8[10616832]{0:T(1024)(128)(4,1)}), s8[4194304]{0:T(1024)(128)(4,1)S(1)}, s32[]{:S(2)}) async-start(s8[10616832]{0:T(1024)(128)(4,1)} %bitcast.52), calls=%async_computation.1 | async-start | bytes 8388608
  41.5 19.1 %collective-permute-start.3 = (bf16[256,1,288]{0,2,1:T(8,128)(2,1)}, bf16[256,1,288]{0,2,1:T(8,128)(2,1)}, u32[]{:S(2)}, u32[]{:S(2)}) collective-permute-start(bf16[256,1,288]{0,2,1:T(8,128)(2,1)} %get-tuple-element.5), channel_id=1, source_target_pairs={{1,0},{2,1},{3,2},{5,4},{6,5},{7,6},{9,8},{10,9},{11,10},{13,12},{... | collective-permute-start | bytes 442376 | tf_op jit(solution)/shard_map/ppermute | solution.py:21
  42.9 17.7 %slice-start.1 = ((s8[10616832]{0:T(1024)(128)(4,1)}), s8[4194304]{0:T(1024)(128)(4,1)S(1)}, s32[]{:S(2)}) async-start(s8[10616832]{0:T(1024)(128)(4,1)} %bitcast.52), calls=%async_computation.2 | async-start | bytes 8388608
  43.0 17.7 %slice-start.2 = ((s8[10616832]{0:T(1024)(128)(4,1)}), s8[2228224]{0:T(1024)(128)(4,1)S(1)}, s32[]{:S(2)}) async-start(s8[10616832]{0:T(1024)(128)(4,1)} %bitcast.52), calls=%async_computation.3 | async-start | bytes 4456448
  43.0 30.1 %collective-permute-start.5 = (bf16[256,1,288]{0,2,1:T(8,128)(2,1)}, bf16[256,1,288]{0,2,1:T(8,128)(2,1)}, u32[]{:S(2)}, u32[]{:S(2)}) collective-permute-start(bf16[256,1,288]{0,2,1:T(8,128)(2,1)} %get-tuple-element.4), channel_id=1, source_target_pairs={{0,1},{1,2},{2,3},{4,5},{5,6},{6,7},{8,9},{9,10},{10,11},{12,13},{... | collective-permute-start | bytes 442376 | tf_op jit(solution)/shard_map/ppermute | solution.py:19
  73.0 21.8 %copy-start.3 = (bf16[256,8,256]{2,1,0:T(8,128)(2,1)S(1)}, bf16[256,8,256]{2,1,0:T(8,128)(2,1)}, u32[]{:S(2)}) copy-start(bf16[256,8,256]{2,1,0:T(8,128)(2,1)} %param.5) | copy-start | bytes 3145732
Sparse Core Ops, SparseCore 0:
  102.8 134.0 all-reduce.1
where the time goes:
time: 247 us
  waiting for transfers between devices  126 us (51%)
  matrix products  81 us (33%)
  starting transfers between devices  16.6 us (7%)
  between operations  14.2 us (6%)
  other arithmetic  4.73 us (2%)
  local copies, waits for them, and re-layouts  4.31 us (2%)
    psum x1, waiting for transfers between devices, local(): lax.psum(local_grad, ('lon', 'lat')) * (1.0 / math.sqrt(total_cells))  126 us
    dot_general x3, matrix products, spread_block(): jnp.einsum('oip,kipq->koiq', rows_in, tiles, preferred_element_type=jnp.f...  47.1 us
    dot_general x3, matrix products, spread_block(): jnp.einsum('bpq,kib->kipq', selector, part_coefs, preferred_element_type=...  19.8 us
    ppermute x3, starting transfers between devices, with_halo(): lax.ppermute(tail, axis, [(i, (i + 1) % count) for i in range(ends)])  10.8 us
    dot_general x1, matrix products, local(): jnp.einsum('koiq,ciq->koc', spread, inputs, preferred_element_type=jnp.fl...  7.76 us
    dot_general x1, matrix products, local(): jnp.einsum('koc,koiq->ciq', mixing, spread, preferred_element_type=jnp.fl...  6.3 us
    ppermute x3, starting transfers between devices, with_halo(): lax.ppermute(head, axis, [((i + 1) % count, i) for i in range(ends)])  5.81 us
  transfers between devices with their start and end apart: 7, of which 1 were waited for; matrix products, arithmetic and copies ran while one was open for 22% of the time, Pallas kernels for 0%

commit v1 on v0

--- a/solution.py
+++ b/solution.py
@@ -64,7 +64,9 @@
     spread = spread_block(padded, coef_pad, 0, lat_rows, 0, lon_cols)
     local_grad = jnp.einsum("koiq,ciq->koc", spread, inputs, preferred_element_type=jnp.float32)
     total_cells = lat_rows * lax.axis_size("lat") * lon_cols * lax.axis_size("lon")
-    weight_grad = lax.psum(local_grad, ("lon", "lat")) * (1.0 / math.sqrt(total_cells))
+    weight_grad = jnp.sum(lax.all_gather(local_grad, ("lon", "lat")), axis=0) * (
+        1.0 / math.sqrt(total_cells)
+    )
     input_grad = jnp.einsum(
         "koc,koiq->ciq", mixing, spread, preferred_element_type=jnp.float32
     ).astype(jnp.bfloat16)

time: 247 us -> 532 us (2.15)
  waiting for transfers between devices: 126 us -> 389 us
  other arithmetic: 4.73 us -> 28 us
    all_gather x0 -> x1, waiting for transfers between devices: none -> 389 us  [local(): lax.all_gather(local_grad, ('lon', 'lat'))]
    psum x1 -> x0, waiting for transfers between devices: 126 us -> none  [local(): lax.psum(local_grad, ('lon', 'lat')) * (1.0 / math.sqrt(total_cells))]
    reduce_sum x0 -> x1, other arithmetic: none -> 23.3 us  [local(): jnp.sum(lax.all_gather(local_grad, ('lon', 'lat')), axis=0)]
  transfers between devices with their start and end apart: 7 -> 7, of which waited for: 1 -> 1; matrix products, arithmetic and copies ran while one was open for 22% -> 11% of each run, Pallas kernels for 0% -> 0%
where the time goes in v1:
time: 532 us
  waiting for transfers between devices  389 us (73%)
  matrix products  81.3 us (15%)
  other arithmetic  28 us (5%)
  starting transfers between devices  15.8 us (3%)
  between operations  14.2 us (3%)
    all_gather x1, waiting for transfers between devices, local(): lax.all_gather(local_grad, ('lon', 'lat'))  389 us
    dot_general x3, matrix products, spread_block(): jnp.einsum('oip,kipq->koiq', rows_in, tiles, preferred_element_type=jnp.f...  47.3 us
    reduce_sum x1, other arithmetic, local(): jnp.sum(lax.all_gather(local_grad, ('lon', 'lat')), axis=0)  23.3 us
    dot_general x3, matrix products, spread_block(): jnp.einsum('bpq,kib->kipq', selector, part_coefs, preferred_element_type=...  19.9 us
  transfers between devices with their start and end apart: 7, of which 1 were waited for; matrix products, arithmetic and copies ran while one was open for 11% of the time, Pallas kernels for 0%

profile of v1, /device:TPU:0, one launch (start us, length us, event | category | flops | bytes accessed | tf_op | source)
XLA Modules:
  0.0 532.0 jit_solution(11151286358783849424)
XLA Ops:
  7.2 0.0 copy-start
  7.2 0.0 all-gather.3.cloned.1.call-start
  7.2 0.8 compare_convert_fusion
  8.0 0.8 broadcast_multiply_fusion.1
  8.9 2.4 collective-permute-start.4
  11.3 1.3 collective-permute-start
  12.6 1.6 copy.13
  14.3 2.4 collective-permute-start.1
  16.6 3.1 collective-permute-start.2
  19.8 1.3 fusion.3
  21.0 6.7 %fusion.7 = bf16[9,8,288,256]{3,1,2,0:T(8,128)(2,1)} fusion(pred[33,288,256,1]{2,1,0,3:T(32,128)(4,1)S(1)} %fusion.3, bf16[9,8,3,33]{3,1,2,0:T(8,128)(2,1)S(1)} %broadcast_multiply_fusion.1), kind=kOutput, calls=%fused_computation.12 | convolution fusion | flops 350355456 | bytes 13068288 | tf_op jit(solution)/shard_map/bpq,kib->kipq/dot_general | solution.py:44
  27.7 0.0 collective-permute-done.4
  27.7 6.6 %fusion.5 = bf16[9,8,288,256]{3,1,2,0:T(8,128)(2,1)} fusion(pred[33,288,256,1]{2,1,0,3:T(32,128)(4,1)S(1)} %fusion.3, bf16[9,8,3,33]{3,1,2,0:T(8,128)(2,1)S(1)} %broadcast_multiply_fusion.1, bf16[9,1,3,33]{3,1,2,0:T(2,128)(2,1)S(1)} %collective-permute-done.4), kind=kOutput, calls=%fused_computation.10 | convolution fusion | flops 350364960 | bytes 13065894 | tf_op jit(solution)/shard_map/bpq,kib->kipq/dot_general | solution.py:44
  34.4 0.0 collective-permute-done
  34.4 6.6 %fusion.9 = bf16[9,8,288,256]{3,1,2,0:T(8,128)(2,1)} fusion(pred[33,288,256,1]{2,1,0,3:T(32,128)(4,1)S(1)} %fusion.3, bf16[9,1,3,33]{3,1,2,0:T(2,128)(2,1)S(1)} %collective-permute-done, bf16[9,8,3,33]{3,1,2,0:T(8,128)(2,1)S(1)} %broadcast_multiply_fusion.1), kind=kOutput, calls=%fused_computation.14 | convolution fusion | flops 350364960 | bytes 13065894 | tf_op jit(solution)/shard_map/bpq,kib->kipq/dot_general | solution.py:44
  40.9 0.0 collective-permute-done.1
  40.9 0.0 collective-permute-done.2
  40.9 0.1 pad_maximum_fusion.10
  41.0 0.0 slice-start
  41.0 0.7 fusion.31
  41.8 4.8 collective-permute-start.5
  46.6 0.0 slice-start.1
  46.6 0.0 slice-start.2
  46.6 1.7 collective-permute-start.3
  48.3 13.1 %fusion.1 = f32[8,9,256,256]{3,2,1,0:T(8,128)} fusion(bf16[9,8,288,256]{3,1,2,0:T(8,128)(2,1)} %fusion.7, bf16[256,8,16]{0,2,1:T(8,128)(2,1)S(1)} %collective-permute-done.2, bf16[256,8,256]{0,2,1:T(8,128)(2,1)S(1)} %copy.13, bf16[256,8,16]{0,2,1:T(8,128)(2,1)S(1)} %collective-permute-done.1), kind=kOutput, calls=%fused_computation.5 | convolution fusion | flops 2721447936 | bytes 30670848 | tf_op jit(solution)/shard_map/oip,kipq->koiq/dot_general | solution.py:47
  61.4 0.0 collective-permute-done.3
  61.4 0.0 slice-done
  61.4 0.0 slice-done.1
  61.4 0.0 slice-done.2
  61.5 12.4 %fusion = f32[8,9,256,256]{3,2,1,0:T(8,128)} fusion(bf16[9,8,288,256]{3,1,2,0:T(8,128)(2,1)S(1)} %bitcast.54, bf16[256,1,288]{0,2,1:T(8,128)(2,1)} %collective-permute-done.3, bf16[256,8,16]{0,2,1:T(8,128)(2,1)S(1)} %collective-permute-done.2, bf16[256,8,256]{0,2,1:T(8,128)(2,1)S(1)} %copy.13, bf16[256,8,16]{0,2,1:T(8,128)(2,1)S(1)} %collective-permute-done.1), kind=kOutput, calls=%fused_computation.4 | convolution fusion | flops 2722627584 | bytes 30818304 | tf_op jit(solution)/shard_map/oip,kipq->koiq/dot_general | solution.py:47
  73.8 0.0 copy-start.1
  73.8 0.0 collective-permute-done.5
  73.8 21.9 %fusion.4 = bf16[9,256,8,256]{1,3,0,2:T(8,128)(2,1)} fusion(f32[8,9,256,256]{3,2,1,0:T(8,128)} %fusion, f32[8,9,256,256]{3,2,1,0:T(8,128)} %fusion.1, bf16[9,8,288,256]{3,1,2,0:T(8,128)(2,1)} %fusion.5, bf16[256,1,288]{0,2,1:T(8,128)(2,1)} %collective-permute-done.5, bf16[256,8,16]{0,2,1:T(8,128)(2,1)S(1)} %collective-permute-done.2, ...), kind=kOutput, calls=%fused_computation.9 | convolution fusion | flops 2736783360 | bytes 59129856 | tf_op jit(solution)/shard_map/oip,kipq->koiq/dot_general | solution.py:47
  95.7 0.0 copy-done.1
  95.7 7.8 %convolution_bitcast_fusion = f32[9,256,256]{2,1,0:T(8,128)} fusion(bf16[9,256,8,256]{1,3,0,2:T(8,128)(2,1)} %fusion.4, bf16[256,8,256,1]{2,1,0,3:T(8,128)(2,1)S(1)} %bitcast.55), kind=kOutput, calls=%fused_computation.17 | convolution fusion | flops 2415919104 | bytes 12845056 | tf_op jit(solution)/shard_map/koiq,ciq->koc/dot_general | solution.py:65
  103.5 0.0 all-gather.3.cloned.1.call-update
  103.5 0.0 copy-done
  103.5 6.3 %fusion.11 = bf16[256,8,256]{0,2,1:T(8,128)(2,1)S(1)} fusion(bf16[9,256,8,256]{1,3,0,2:T(8,128)(2,1)} %fusion.4, bf16[9,256,256]{2,1,0:T(8,128)(2,1)S(1)} %copy-done), kind=kOutput, calls=%fused_computation.18 | convolution fusion | flops 2416443392 | bytes 11665408 | tf_op jit(solution)/shard_map/koc,koiq->ciq/dot_general | solution.py:70
  109.8 1.8 copy.18
  111.6 388.6 %all-gather.3.cloned.1.call-done = f32[288,256,256]{2,1,0:T(8,128)} async-done(((f32[9,256,256]{2,1,0:T(8,128)}), f32[288,256,256]{2,1,0:T(8,128)}) %all-gather.3.cloned.1.call-update) | async-done | bytes 75497488 | tf_op jit(solution)/shard_map/all_gather | solution.py:67
  500.2 23.3 %reduce_sum.9 = f32[9,256,256]{2,1,0:T(8,128)S(1)} reduce(f32[32,9,256,256]{3,2,1,0:T(8,128)} %bitcast.23, f32[]{:T(128)} %constant.3.clone.1), dimensions={0}, to_apply=%region_0.0 | reduce | flops 18284544 | bytes 77856768 | tf_op jit(solution)/shard_map/reduce_sum | solution.py:67
  523.5 1.6 broadcast_multiply_fusion
  (6 shorter events, 0.1 us)
Async XLA Ops:
  7.2 96.3 %copy-start = (bf16[9,256,256]{2,1,0:T(8,128)(2,1)S(1)}, bf16[9,256,256]{2,1,0:T(8,128)(2,1)}, u32[]{:S(2)}) copy-start(bf16[9,256,256]{2,1,0:T(8,128)(2,1)} %param.7) | copy-start | bytes 3538948
  7.2 493.0 %all-gather.3.cloned.1.call-start = ((), (), s32[]{:S(2)}) async-start(), calls=%async_computation | async-start | bytes 77856768 | tf_op jit(solution)/shard_map/all_gather | solution.py:67
  8.9 18.8 %collective-permute-start.4 = (bf16[9,1,3,33]{3,1,2,0:T(2,128)(2,1)S(1)}, bf16[9,1,3,33]{3,1,2,0:T(2,128)(2,1)S(1)}, u32[]{:S(2)}, u32[]{:S(2)}) collective-permute-start(bf16[9,1,3,33]{3,1,2,0:T(2,128)(2,1)S(1)} %get-tuple-element.10), channel_id=1, source_target_pairs={{0,1},{1,2},{2,3},{4,5},{5,6},{6,7},{8,9},{9,10},{10,11},{12,13},{... | collective-permute-start | bytes 5354 | tf_op jit(solution)/shard_map/ppermute | solution.py:19
  11.3 23.1 %collective-permute-start = (bf16[9,1,3,33]{3,1,2,0:T(2,128)(2,1)S(1)}, bf16[9,1,3,33]{3,1,2,0:T(2,128)(2,1)S(1)}, u32[]{:S(2)}, u32[]{:S(2)}) collective-permute-start(bf16[9,1,3,33]{3,1,2,0:T(2,128)(2,1)S(1)} %get-tuple-element.11), channel_id=1, source_target_pairs={{1,0},{2,1},{3,2},{5,4},{6,5},{7,6},{9,8},{10,9},{11,10},{13,12},{... | collective-permute-start | bytes 5354 | tf_op jit(solution)/shard_map/ppermute | solution.py:21
  14.3 26.7 %collective-permute-start.1 = (bf16[256,8,16]{0,2,1:T(8,128)(2,1)S(1)}, bf16[256,8,16]{0,2,1:T(8,128)(2,1)S(1)}, u32[]{:S(2)}, u32[]{:S(2)}) collective-permute-start(bf16[256,8,16]{0,2,1:T(8,128)(2,1)S(1)} %get-tuple-element.8), channel_id=1, source_target_pairs={{0,4},{4,8},{8,12},{12,16},{16,20},{20,24},{24,28},{28,0},{1,5},{5... | collective-permute-start | bytes 196616 | tf_op jit(solution)/shard_map/ppermute | solution.py:19
  16.6 24.3 %collective-permute-start.2 = (bf16[256,8,16]{0,2,1:T(8,128)(2,1)S(1)}, bf16[256,8,16]{0,2,1:T(8,128)(2,1)S(1)}, u32[]{:S(2)}, u32[]{:S(2)}) collective-permute-start(bf16[256,8,16]{0,2,1:T(8,128)(2,1)S(1)} %get-tuple-element.9), channel_id=1, source_target_pairs={{4,0},{8,4},{12,8},{16,12},{20,16},{24,20},{28,24},{0,28},{5,1},{9... | collective-permute-start | bytes 196616 | tf_op jit(solution)/shard_map/ppermute | solution.py:21
  41.0 20.4 %slice-start = ((s8[10616832]{0:T(1024)(128)(4,1)}), s8[4194304]{0:T(1024)(128)(4,1)S(1)}, s32[]{:S(2)}) async-start(s8[10616832]{0:T(1024)(128)(4,1)} %bitcast.53), calls=%async_computation.1 | async-start | bytes 8388608
  41.8 32.1 %collective-permute-start.5 = (bf16[256,1,288]{0,2,1:T(8,128)(2,1)}, bf16[256,1,288]{0,2,1:T(8,128)(2,1)}, u32[]{:S(2)}, u32[]{:S(2)}) collective-permute-start(bf16[256,1,288]{0,2,1:T(8,128)(2,1)} %get-tuple-element.6), channel_id=1, source_target_pairs={{0,1},{1,2},{2,3},{4,5},{5,6},{6,7},{8,9},{9,10},{10,11},{12,13},{... | collective-permute-start | bytes 442376 | tf_op jit(solution)/shard_map/ppermute | solution.py:19
  46.6 14.8 %slice-start.1 = ((s8[10616832]{0:T(1024)(128)(4,1)}), s8[4194304]{0:T(1024)(128)(4,1)S(1)}, s32[]{:S(2)}) async-start(s8[10616832]{0:T(1024)(128)(4,1)} %bitcast.53), calls=%async_computation.2 | async-start | bytes 8388608
  46.6 14.8 %slice-start.2 = ((s8[10616832]{0:T(1024)(128)(4,1)}), s8[2228224]{0:T(1024)(128)(4,1)S(1)}, s32[]{:S(2)}) async-start(s8[10616832]{0:T(1024)(128)(4,1)} %bitcast.53), calls=%async_computation.3 | async-start | bytes 4456448
  46.6 14.8 %collective-permute-start.3 = (bf16[256,1,288]{0,2,1:T(8,128)(2,1)}, bf16[256,1,288]{0,2,1:T(8,128)(2,1)}, u32[]{:S(2)}, u32[]{:S(2)}) collective-permute-start(bf16[256,1,288]{0,2,1:T(8,128)(2,1)} %get-tuple-element.7), channel_id=1, source_target_pairs={{1,0},{2,1},{3,2},{5,4},{6,5},{7,6},{9,8},{10,9},{11,10},{13,12},{... | collective-permute-start | bytes 442376 | tf_op jit(solution)/shard_map/ppermute | solution.py:21
  73.8 21.9 %copy-start.1 = (bf16[256,8,256]{2,1,0:T(8,128)(2,1)S(1)}, bf16[256,8,256]{2,1,0:T(8,128)(2,1)}, u32[]{:S(2)}) copy-start(bf16[256,8,256]{2,1,0:T(8,128)(2,1)} %param.5) | copy-start | bytes 3145732
Sparse Core Ops, SparseCore 0:
  103.6 396.5 all-gather.2
